TPU v7x, 256 devices: a whole 4x4x8 slice. The times are simulated.
256 devices in a mesh: row: 32 (over z, y_hi, core), col: 8 (over x, y_lo).
Axes of the slice: x: 4, y: 4 (y_hi: 2, y_lo: 2; y = y_hi * 2 + y_lo), z: 8, core: 2. Of those that a mesh axis runs over, the one named last changes fastest.
Arguments:
- feature_map: bfloat16 [256, 256, 384], P('row', 'col'), may hold values from -6 to 6
- kernel: float32 [7, 7, 384], replicated, may hold values from -0.875 to 0.875
- ln_gain: float32 [384], replicated, may hold values from 0.5 to 1.5
- ln_bias: float32 [384], replicated, may hold values from -3 to 3
- w_in: bfloat16 [384, 1536], P(None, ('row', 'col')), may hold values from -0.3125 to 0.3125
- b_in: float32 [1536], replicated, may hold values from -3 to 3
- w_out: bfloat16 [1536, 384], P(('row', 'col')), may hold values from -0.15625 to 0.15625
- b_out: float32 [384], replicated, may hold values from -3 to 3
- layer_scale: float32 [384], replicated, may hold values from 0.5 to 1.5
- cotangent: bfloat16 [256, 256, 384], P('row', 'col'), may hold values from -6 to 6
Outputs:
- block_out: bfloat16 [256, 256, 384], P('row', 'col')
- grad_input: bfloat16 [256, 256, 384], P('row', 'col')
- grad_w_in: float32 [384, 1536], P(None, ('row', 'col'))
- grad_w_out: float32 [1536, 384], P(('row', 'col'))
- small_grads: float32 [53, 384], replicated
- grad_b_in: float32 [1536], replicated
All inputs are finite; a program needn't handle non-finite values.
Results may differ from a plain program's by a relative error of at most 0.007.
Values may be sent and summed in bfloat16 or wider, within the bound.
No kernel may reach another device: no remote copies, remote signals or barrier semaphores. Data moves between devices by JAX's collectives and lax.ppermute only.
A program may use at most 64 MiB of HBM per device.

v0:
```python
import math
import jax
import jax.numpy as jnp
from jax import lax
from jax.sharding import PartitionSpec as P


def padded_2(x, sides, width):
    for axis, dim in sides:
        peers, length = (lax.axis_size(axis), x.shape[dim])
        up = [(i, (i + 1) % peers) for i in range(peers - 1)]
        down = [(j, i) for i, j in up]
        last = lax.slice_in_dim(x, length - width, length, axis=dim)
        first = lax.slice_in_dim(x, 0, width, axis=dim)
        before = lax.ppermute(last, axis, up)
        after = lax.ppermute(first, axis, down)
        x = jnp.concatenate([before, x, after], axis=dim)
    return x


def gelu_parts(hidden):
    normal_cdf = 0.5 * (1.0 + jax.scipy.special.erf(hidden * (1.0 / math.sqrt(2.0))))
    density = jnp.exp(-0.5 * hidden * hidden) * (1.0 / math.sqrt(2.0 * math.pi))
    return (hidden * normal_cdf, normal_cdf + hidden * density)


def extend(field):
    return padded_2(field, (("row", 0), ("col", 1)), 3)


def on_device(
    feature_map, kernel, ln_gain, ln_bias, w_in, b_in, w_out, b_out, layer_scale, cotangent
):
    row_count, col_count, channels = feature_map.shape
    pixels = row_count * col_count
    padded = extend(feature_map).astype(jnp.float32)
    conv = jnp.zeros((row_count, col_count, channels), jnp.float32)
    for tap_row in range(7):
        for tap_col in range(7):
            conv = (
                conv
                + padded[tap_row : tap_row + row_count, tap_col : tap_col + col_count]
                * kernel[tap_row, tap_col]
            )
    average = jnp.mean(conv, -1, keepdims=True)
    centered = conv - average
    variance = jnp.mean(centered * centered, -1, keepdims=True)
    inv_std = lax.rsqrt(variance + 1e-06)
    unit_scaled = centered * inv_std
    normed = (unit_scaled * ln_gain + ln_bias).astype(jnp.bfloat16).reshape(pixels, channels)
    contract_last = (((1,), (1,)), ((), ()))
    contract_first = (((0,), (0,)), ((), ()))
    w_in_full = lax.all_gather(w_in, ("row", "col"), axis=1, tiled=True)
    w_out_full = lax.all_gather(w_out, ("row", "col"), axis=0, tiled=True)
    hidden = jnp.dot(normed, w_in_full, preferred_element_type=jnp.float32) + b_in
    act_value, slope = gelu_parts(hidden)
    activated = act_value.astype(jnp.bfloat16)
    mixed = jnp.dot(activated, w_out_full, preferred_element_type=jnp.float32) + b_out
    source = feature_map.astype(jnp.float32).reshape(pixels, channels)
    block_out = (
        (source + layer_scale * mixed).astype(jnp.bfloat16).reshape(row_count, col_count, channels)
    )
    grad_flow = cotangent.astype(jnp.float32).reshape(pixels, channels)
    grad_mixed = grad_flow * layer_scale
    mixed_low = grad_mixed.astype(jnp.bfloat16)
    grad_act = lax.dot_general(
        mixed_low, w_out_full, contract_last, preferred_element_type=jnp.float32
    )
    grad_hidden = (grad_act * slope).astype(jnp.bfloat16)
    grad_w_out = lax.psum_scatter(
        lax.dot_general(activated, mixed_low, contract_first, preferred_element_type=jnp.float32),
        ("row", "col"),
        scatter_dimension=0,
        tiled=True,
    )
    win_term = lax.dot_general(
        normed, grad_hidden, contract_first, preferred_element_type=jnp.float32
    )
    grad_w_in = lax.psum_scatter(win_term, ("row", "col"), scatter_dimension=1, tiled=True)
    grad_normed = lax.dot_general(
        grad_hidden, w_in_full, contract_last, preferred_element_type=jnp.float32
    )
    grad_normed = grad_normed.reshape(row_count, col_count, channels)
    grad_gain = jnp.sum(grad_normed * unit_scaled, (0, 1))
    grad_lnb = jnp.sum(grad_normed, (0, 1))
    scaled_grad = grad_normed * ln_gain
    grad_conv = inv_std * (
        scaled_grad
        - jnp.mean(scaled_grad, -1, keepdims=True)
        - unit_scaled * jnp.mean(scaled_grad * unit_scaled, -1, keepdims=True)
    )
    tap_terms = []
    for tap_row in range(7):
        for tap_col in range(7):
            tap_terms.append(
                jnp.sum(
                    padded[tap_row : tap_row + row_count, tap_col : tap_col + col_count]
                    * grad_conv,
                    (0, 1),
                )
            )
    grad_pad = extend(grad_conv.astype(jnp.bfloat16)).astype(jnp.float32)
    back_conv = jnp.zeros((row_count, col_count, channels), jnp.float32)
    for tap_row in range(7):
        for tap_col in range(7):
            back_conv = (
                back_conv
                + grad_pad[
                    6 - tap_row : 6 - tap_row + row_count, 6 - tap_col : 6 - tap_col + col_count
                ]
                * kernel[tap_row, tap_col]
            )
    grad_input = (cotangent.astype(jnp.float32) + back_conv).astype(jnp.bfloat16)
    small_local = jnp.concatenate(
        [
            jnp.stack(tap_terms, 0),
            grad_gain[None],
            grad_lnb[None],
            jnp.sum(grad_mixed, 0)[None],
            jnp.sum(grad_flow * mixed, 0)[None],
        ],
        0,
    )
    bias_local = jnp.sum(grad_hidden.astype(jnp.float32), 0)
    small_grads, grad_b_in = lax.psum((small_local, bias_local), ("row", "col"))
    return (block_out, grad_input, grad_w_in, grad_w_out, small_grads, grad_b_in)


def solution(mesh):
    placed = (
        P("row", "col", None),
        P(),
        P(),
        P(),
        P(None, ("row", "col")),
        P(),
        P(("row", "col"), None),
        P(),
        P(),
        P("row", "col", None),
    )
    return jax.shard_map(
        on_device,
        mesh=mesh,
        in_specs=placed,
        out_specs=(
            P("row", "col", None),
            P("row", "col", None),
            P(None, ("row", "col")),
            P(("row", "col"), None),
            P(),
            P(),
        ),
        check_vma=False,
    )
```

profile of v0, /device:TPU:99, one launch (start us, length us, event | category | flops | bytes accessed | tf_op | source)
XLA Modules:
  0.0 1693.0 jit_solution(1590831697639832717)
XLA Ops:
  7.9 0.9 fusion.63
  8.9 5.4 collective-permute-start
  14.3 1.9 collective-permute-start.1
  16.3 1.1 slice_reduce_fusion.47
  17.4 1.0 fusion.56
  18.4 1.2 slice_reduce_fusion.48
  19.7 1.0 constant_dynamic-update-slice_fusion.1
  21.5 2.3 collective-permute-start.3
  23.8 3.0 collective-permute-start.2
  26.8 1.0 slice_reduce_fusion.46
  28.5 1.0 collective-permute-done.2
  29.6 3.2 fusion.60
  33.3 671.1 %all-gather.5.cloned.1.call-done = bf16[256,6,384]{2,1,0:T(8,128)(2,1)} async-done(((bf16[1,6,384]{2,1,0:T(8,128)(2,1)}), bf16[256,6,384]{2,1,0:T(8,128)(2,1)}) %all-gather.5.cloned.1.call-update) | async-done | bytes 1179664 | tf_op jit(solution)/shard_map/all_gather | solution.py:53
  704.4 2.3 reshape.74
  706.7 2.5 multiply_convert_fusion
  709.2 684.3 %all-gather.7.cloned.1.call-done = bf16[256,6,384]{2,1,0:T(8,128)(2,1)} async-done(((bf16[1,6,384]{2,1,0:T(8,128)(2,1)}), bf16[256,6,384]{2,1,0:T(8,128)(2,1)}) %all-gather.7.cloned.1.call-update) | async-done | bytes 1179664 | tf_op jit(solution)/shard_map/all_gather | solution.py:54
  1393.6 3.3 reshape.76
  1396.8 3.5 fusion.58
  1400.3 0.9 convert_reduce_fusion
  1401.9 2.0 fusion.64
  1404.0 2.1 fusion.65
  1409.2 4.4 concatenate.19
  1413.8 1.9 collective-permute-start.5
  1415.7 5.1 collective-permute-start.4
  1422.3 1.9 collective-permute-start.7
  1424.3 3.4 collective-permute-start.6
  1427.6 73.7 %psum.15 = f32[1536]{0:T(1024)} all-reduce(f32[1536]{0:T(1024)S(1)} %get-tuple-element.129), channel_id=1, replica_groups=mesh['row'=32,'col'=8] {'row','col'}, use_global_device_ids=true, to_apply=%region_61.0 | all-reduce | flops 1536 | bytes 12288 | tf_op jit(solution)/shard_map/psum | solution.py:125
  1501.7 3.5 fusion.7
  1505.2 177.1 %all-reduce.5.cloned.1.call-done = (f32[384,1536]{0,1:T(8,128)}, f32[1536,384]{1,0:T(8,128)}, f32[53,384]{1,0:T(8,128)}) async-done(((f32[384,1536]{0,1:T(8,128)}, f32[1536,384]{1,0:T(8,128)}, f32[53,384]{1,0:T(8,128)}), (f32[384,1536]{0,1:T(8,128)}, f32[1536,384]{1,0:T(8,128)}, f32[53,384]{1,0:T(8,128)})) %all-reduce.5.cloned.1.call-update) | async-done | bytes 4800016
  1682.2 1.3 constant_dynamic-slice_fusion.1
  1683.6 1.3 constant_dynamic-slice_fusion
  1684.9 1.5 copy.21
  (173 shorter events, 7.8 us)
Async XLA Ops:
  7.2 697.2 %all-gather.5.cloned.1.call-start = ((), (), s32[]{:S(2)}) async-start(), calls=%async_computation | async-start | bytes 1579008 | tf_op jit(solution)/shard_map/all_gather | solution.py:53
  7.9 1385.7 %all-gather.7.cloned.1.call-start = ((), (), s32[]{:S(2)}) async-start(), calls=%async_computation.1 | async-start | bytes 1579008 | tf_op jit(solution)/shard_map/all_gather | solution.py:54
  8.9 10.8 collective-permute-start
  14.3 7.2 collective-permute-start.1
  16.2 1666.0 %all-reduce.5.cloned.1.call-start = ((), (), s32[]{:S(2)}) async-start(), calls=%async_computation.2 | async-start | bytes 9609216
  19.6 13.2 copy-start.5
  19.6 13.1 copy-start.7
  21.5 6.9 collective-permute-start.3
  23.8 5.7 collective-permute-start.2
  709.2 691.1 %copy-start = (bf16[256,1536]{1,0:T(8,128)(2,1)}, bf16[256,1536]{1,0:T(8,128)(2,1)S(1)}, u32[]{:S(2)}) copy-start(bf16[256,1536]{1,0:T(8,128)(2,1)S(1)} %get-tuple-element.126) | copy-start | bytes 2359300
  1413.6 87.9 %copy-start.4 = (bf16[8,32,384]{2,1,0:T(8,128)(2,1)S(1)}, bf16[8,32,384]{2,1,0:T(8,128)(2,1)}, u32[]{:S(2)}) copy-start(bf16[8,32,384]{2,1,0:T(8,128)(2,1)} %param.19) | copy-start | bytes 589828
  1413.6 87.9 %copy-start.6 = (f32[384]{0:T(512)S(1)}, f32[384]{0:T(512)}, u32[]{:S(2)}) copy-start(f32[384]{0:T(512)} %copy-done.5) | copy-start | bytes 4612
  1413.6 87.9 %copy-start.8 = (f32[384]{0:T(512)S(1)}, f32[384]{0:T(512)}, u32[]{:S(2)}) copy-start(f32[384]{0:T(512)} %copy-done.7) | copy-start | bytes 4612
  1413.6 87.9 %copy-start.10 = (f32[384]{0:T(512)S(1)}, f32[384]{0:T(512)}, u32[]{:S(2)}) copy-start(f32[384]{0:T(512)} %copy-done.9) | copy-start | bytes 4612
  1413.6 87.9 %copy-start.12 = (f32[384]{0:T(512)S(1)}, f32[384]{0:T(512)}, u32[]{:S(2)}) copy-start(f32[384]{0:T(512)} %copy-done.11) | copy-start | bytes 4612
  1413.7 87.9 %copy-start.14 = (f32[384]{0:T(512)S(1)}, f32[384]{0:T(512)}, u32[]{:S(2)}) copy-start(f32[384]{0:T(512)} %copy-done.13) | copy-start | bytes 4612
  1413.7 87.9 %copy-start.16 = (f32[384]{0:T(512)S(1)}, f32[384]{0:T(512)}, u32[]{:S(2)}) copy-start(f32[384]{0:T(512)} %copy-done.15) | copy-start | bytes 4612
  1413.7 87.9 %copy-start.18 = (f32[384]{0:T(512)S(1)}, f32[384]{0:T(512)}, u32[]{:S(2)}) copy-start(f32[384]{0:T(512)} %copy-done.17) | copy-start | bytes 4612
  1413.7 87.9 %copy-start.20 = (f32[384]{0:T(512)S(1)}, f32[384]{0:T(512)}, u32[]{:S(2)}) copy-start(f32[384]{0:T(512)} %copy-done.19) | copy-start | bytes 4612
  1413.7 87.9 %copy-start.22 = (f32[384]{0:T(512)S(1)}, f32[384]{0:T(512)}, u32[]{:S(2)}) copy-start(f32[384]{0:T(512)} %copy-done.21) | copy-start | bytes 4612
  1413.7 87.9 %copy-start.24 = (f32[384]{0:T(512)S(1)}, f32[384]{0:T(512)}, u32[]{:S(2)}) copy-start(f32[384]{0:T(512)} %copy-done.23) | copy-start | bytes 4612
  1413.7 87.9 %copy-start.26 = (f32[384]{0:T(512)S(1)}, f32[384]{0:T(512)}, u32[]{:S(2)}) copy-start(f32[384]{0:T(512)} %copy-done.25) | copy-start | bytes 4612
  1413.7 87.9 %copy-start.28 = (f32[384]{0:T(512)S(1)}, f32[384]{0:T(512)}, u32[]{:S(2)}) copy-start(f32[384]{0:T(512)} %copy-done.27) | copy-start | bytes 4612
  1413.7 87.9 %copy-start.30 = (f32[384]{0:T(512)S(1)}, f32[384]{0:T(512)}, u32[]{:S(2)}) copy-start(f32[384]{0:T(512)} %copy-done.29) | copy-start | bytes 4612
  1413.7 87.9 %copy-start.32 = (f32[384]{0:T(512)S(1)}, f32[384]{0:T(512)}, u32[]{:S(2)}) copy-start(f32[384]{0:T(512)} %copy-done.31) | copy-start | bytes 4612
  1413.8 87.9 %copy-start.34 = (f32[384]{0:T(512)S(1)}, f32[384]{0:T(512)}, u32[]{:S(2)}) copy-start(f32[384]{0:T(512)} %copy-done.33) | copy-start | bytes 4612
  1413.8 87.9 %copy-start.36 = (f32[384]{0:T(512)S(1)}, f32[384]{0:T(512)}, u32[]{:S(2)}) copy-start(f32[384]{0:T(512)} %copy-done.35) | copy-start | bytes 4612
  1413.8 87.9 %copy-start.38 = (f32[384]{0:T(512)S(1)}, f32[384]{0:T(512)}, u32[]{:S(2)}) copy-start(f32[384]{0:T(512)} %copy-done.37) | copy-start | bytes 4612
  1413.8 7.6 collective-permute-start.5
  1415.7 6.5 collective-permute-start.4
  1422.3 79.0 %collective-permute-start.7 = (bf16[14,3,384]{2,1,0:T(4,128)(2,1)S(1)}, bf16[14,3,384]{2,1,0:T(4,128)(2,1)S(1)}, u32[]{:S(2)}, u32[]{:S(2)}) collective-permute-start(bf16[14,3,384]{2,1,0:T(4,128)(2,1)S(1)} %get-tuple-element.118), channel_id=1, source_target_pairs={{1,0},{2,1},{3,2},{4,3},{5,4},{6,5},{7,6},{9,8},{10,9},{11,10},{12... | collective-permute-start | bytes 96776 | tf_op jit(solution)/shard_map/ppermute | solution.py:16
  1424.3 77.1 %collective-permute-start.6 = (bf16[14,3,384]{2,1,0:T(4,128)(2,1)S(1)}, bf16[14,3,384]{2,1,0:T(4,128)(2,1)S(1)}, u32[]{:S(2)}, u32[]{:S(2)}) collective-permute-start(bf16[14,3,384]{2,1,0:T(4,128)(2,1)S(1)} %get-tuple-element.117), channel_id=1, source_target_pairs={{0,1},{1,2},{2,3},{3,4},{4,5},{5,6},{6,7},{8,9},{9,10},{10,11},{11... | collective-permute-start | bytes 96776 | tf_op jit(solution)/shard_map/ppermute | solution.py:15
  (23 other events, 127.4 us)
Sparse Core Ops, SparseCore 0:
  9.9 694.4 all-gather.4
  706.3 687.2 all-gather.6
  1413.7 268.4 all-reduce.4
where the time goes:
time: 1690 us
  waiting for transfers between devices  1540 us (91%)
  blocking collectives  73.7 us (4%)
  starting transfers between devices  25.1 us (1%)
  local copies, waits for them, and re-layouts  20.5 us (1%)
    all_gather x1, waiting for transfers between devices, on_device(): w_out_full = lax.all_gather(w_out, ('row', 'col'), axis=0, tiled=True)  684 us
    all_gather x1, waiting for transfers between devices, on_device(): w_in_full = lax.all_gather(w_in, ('row', 'col'), axis=1, tiled=True)  671 us
    unnamed x4, waiting for transfers between devices  178 us
    psum x1, blocking collectives, on_device(): small_grads, grad_b_in = lax.psum((small_local, bias_local), ('row', 'col'))  73.7 us
  transfers between devices with their start and end apart: 11, of which 7 were waited for; matrix products, arithmetic and copies ran while one was open for 1% of the time, Pallas kernels for 0%

commit v1 on v0

--- a/solution.py
+++ b/solution.py
@@ -50,7 +50,10 @@
     normed = (unit_scaled * ln_gain + ln_bias).astype(jnp.bfloat16).reshape(pixels, channels)
     contract_last = (((1,), (1,)), ((), ()))
     contract_first = (((0,), (0,)), ((), ()))
-    w_in_full = lax.all_gather(w_in, ("row", "col"), axis=1, tiled=True)
+    w_in_full = jnp.concatenate(
+        lax.all_to_all(jnp.stack([w_in] * lax.axis_size(("row", "col"))), ("row", "col"), 0, 0),
+        axis=1,
+    )
     w_out_full = lax.all_gather(w_out, ("row", "col"), axis=0, tiled=True)
     hidden = jnp.dot(normed, w_in_full, preferred_element_type=jnp.float32) + b_in
     act_value, slope = gelu_parts(hidden)

time: 1690 us -> 1030 us (0.61)
  waiting for transfers between devices: 1540 us -> 862 us
    all_gather x1 -> x0, waiting for transfers between devices: 671 us -> none  [on_device(): w_in_full = lax.all_gather(w_in, ('row', 'col'), axis=1, tiled=True)]
    all_gather x1, waiting for transfers between devices: 684 us -> 656 us  [on_device(): w_out_full = lax.all_gather(w_out, ('row', 'col'), axis=0, tiled=True)]
    all_to_all x0 -> x1, waiting for transfers between devices: none -> 24.4 us  [on_device(): lax.all_to_all(jnp.stack([w_in] * lax.axis_size(('row', 'col'))), ('row',...]
    unnamed x4 -> x3, waiting for transfers between devices: 178 us -> 177 us
  transfers between devices with their start and end apart: 11 -> 11, of which waited for: 7 -> 6; matrix products, arithmetic and copies ran while one was open for 1% -> 1% of each run, Pallas kernels for 0% -> 0%
where the time goes in v1:
time: 1030 us
  waiting for transfers between devices  862 us (84%)
  blocking collectives  74.1 us (7%)
  starting transfers between devices  39.8 us (4%)
  local copies, waits for them, and re-layouts  17.6 us (2%)
  between operations  15.3 us (1%)
  matrix products  11.3 us (1%)
    all_gather x1, waiting for transfers between devices, on_device(): w_out_full = lax.all_gather(w_out, ('row', 'col'), axis=0, tiled=True)  656 us
    unnamed x3, waiting for transfers between devices  177 us
    psum x1, blocking collectives, on_device(): small_grads, grad_b_in = lax.psum((small_local, bias_local), ('row', 'col'))  74.1 us
    all_to_all x1, waiting for transfers between devices, on_device(): lax.all_to_all(jnp.stack([w_in] * lax.axis_size(('row', 'col'))), ('row',...  24.4 us
  transfers between devices with their start and end apart: 11, of which 6 were waited for; matrix products, arithmetic and copies ran while one was open for 1% of the time, Pallas kernels for 0%

profile of v1, /device:TPU:99, one launch (start us, length us, event | category | flops | bytes accessed | tf_op | source)
XLA Modules:
  0.0 1030.0 jit_solution(15613391668484383528)
XLA Ops:
  7.2 0.9 fusion.64
  8.1 5.4 collective-permute-start
  13.5 1.9 collective-permute-start.1
  15.4 2.0 stack.100
  17.4 14.6 %all-to-all-start = ((bf16[256,384,6]{1,2,0:T(8,128)(2,1)}), bf16[256,384,6]{1,2,0:T(8,128)(2,1)S(1)}, u32[]{:S(2)}, u32[]{:S(2)}) async-start(bf16[256,384,6]{1,2,0:T(8,128)(2,1)} %stack.100), calls=%async_computation | async-start | bytes 3145728 | tf_op jit(solution)/shard_map/all_to_all | solution.py:54
  33.3 3.1 collective-permute-start.3
  36.4 2.1 collective-permute-start.2
  39.3 3.2 collective-permute-done.2
  42.7 3.2 fusion.61
  46.4 24.4 %all-to-all-done = bf16[256,384,6]{1,2,0:T(8,128)(2,1)S(1)} async-done(((bf16[256,384,6]{1,2,0:T(8,128)(2,1)}), bf16[256,384,6]{1,2,0:T(8,128)(2,1)S(1)}, u32[]{:S(2)}, u32[]{:S(2)}) %all-to-all-start) | async-done | bytes 1179680 | tf_op jit(solution)/shard_map/all_to_all | solution.py:54
  70.8 1.3 reshape.70
  72.0 3.1 multiply_convert_fusion
  75.1 656.1 %all-gather.3.cloned.1.call-done = bf16[256,6,384]{2,1,0:T(8,128)(2,1)} async-done(((bf16[1,6,384]{2,1,0:T(8,128)(2,1)}), bf16[256,6,384]{2,1,0:T(8,128)(2,1)}) %all-gather.3.cloned.1.call-update) | async-done | bytes 1179664 | tf_op jit(solution)/shard_map/all_gather | solution.py:57
  731.3 3.3 reshape.76
  734.6 2.6 fusion.60
  737.1 2.0 fusion.66
  739.4 0.9 convert_reduce_fusion
  740.3 2.0 fusion.65
  743.0 0.9 multiply_reduce_fusion.1
  743.9 0.7 multiply_reduce_fusion.19
  745.8 4.4 concatenate.19
  750.4 1.9 collective-permute-start.5
  752.4 5.1 collective-permute-start.4
  758.0 0.9 collective-permute-done.4
  758.9 1.9 collective-permute-start.7
  760.9 3.5 collective-permute-start.6
  764.4 74.1 %psum.15 = f32[1536]{0:T(1024)} all-reduce(f32[1536]{0:T(1024)S(1)} %get-tuple-element.129), channel_id=1, replica_groups=mesh['row'=32,'col'=8] {'row','col'}, use_global_device_ids=true, to_apply=%region_61.0 | all-reduce | flops 1536 | bytes 12288 | tf_op jit(solution)/shard_map/psum | solution.py:128
  838.8 3.5 fusion.9
  842.3 176.7 %all-reduce.5.cloned.1.call-done = (f32[384,1536]{0,1:T(8,128)}, f32[1536,384]{1,0:T(8,128)}, f32[53,384]{1,0:T(8,128)}) async-done(((f32[384,1536]{0,1:T(8,128)}, f32[1536,384]{1,0:T(8,128)}, f32[53,384]{1,0:T(8,128)}), (f32[384,1536]{0,1:T(8,128)}, f32[1536,384]{1,0:T(8,128)}, f32[53,384]{1,0:T(8,128)})) %all-reduce.5.cloned.1.call-update) | async-done | bytes 4800016
  1019.0 1.3 constant_dynamic-slice_fusion.1
  1020.3 1.3 constant_dynamic-slice_fusion
  1021.7 1.5 copy.26
  (176 shorter events, 4.7 us)
Async XLA Ops:
  8.1 25.0 %collective-permute-start = (bf16[3,32,384]{2,1,0:T(8,128)(2,1)S(1)}, bf16[3,32,384]{2,1,0:T(8,128)(2,1)S(1)}, u32[]{:S(2)}, u32[]{:S(2)}) collective-permute-start(bf16[3,32,384]{2,1,0:T(8,128)(2,1)S(1)} %get-tuple-element.125), channel_id=1, source_target_pairs={{0,8},{8,16},{16,24},{24,32},{32,40},{40,48},{48,56},{56,64},{64,7... | collective-permute-start | bytes 221192 | tf_op jit(solution)/shard_map/ppermute | solution.py:15
  13.5 19.7 %collective-permute-start.1 = (bf16[3,32,384]{2,1,0:T(8,128)(2,1)S(1)}, bf16[3,32,384]{2,1,0:T(8,128)(2,1)S(1)}, u32[]{:S(2)}, u32[]{:S(2)}) collective-permute-start(bf16[3,32,384]{2,1,0:T(8,128)(2,1)S(1)} %get-tuple-element.124), channel_id=1, source_target_pairs={{8,0},{16,8},{24,16},{32,24},{40,32},{48,40},{56,48},{64,56},{72,6... | collective-permute-start | bytes 221192 | tf_op jit(solution)/shard_map/ppermute | solution.py:16
  17.4 15.5 %copy-start.44 = (f32[384]{0:T(512)S(1)}, f32[384]{0:T(512)}, u32[]{:S(2)}) copy-start(f32[384]{0:T(512)} %param.18) | copy-start | bytes 4612
  17.4 15.8 %copy-start.4 = (bf16[8,32,384]{2,1,0:T(8,128)(2,1)S(1)}, bf16[8,32,384]{2,1,0:T(8,128)(2,1)}, u32[]{:S(2)}) copy-start(bf16[8,32,384]{2,1,0:T(8,128)(2,1)} %param.10) | copy-start | bytes 589828
  17.4 53.4 %all-to-all-start = ((bf16[256,384,6]{1,2,0:T(8,128)(2,1)}), bf16[256,384,6]{1,2,0:T(8,128)(2,1)S(1)}, u32[]{:S(2)}, u32[]{:S(2)}) async-start(bf16[256,384,6]{1,2,0:T(8,128)(2,1)} %stack.100), calls=%async_computation | async-start | bytes 3145728 | tf_op jit(solution)/shard_map/all_to_all | solution.py:54
  32.0 699.3 %all-gather.3.cloned.1.call-start = ((), (), s32[]{:S(2)}) async-start(), calls=%async_computation.1 | async-start | bytes 1579008 | tf_op jit(solution)/shard_map/all_gather | solution.py:57
  32.7 986.2 %all-reduce.5.cloned.1.call-start = ((), (), s32[]{:S(2)}) async-start(), calls=%async_computation.2 | async-start | bytes 9609216
  33.3 6.0 collective-permute-start.3
  36.4 6.1 collective-permute-start.2
  75.1 659.4 %copy-start.45 = (f32[384]{0:T(512)S(1)}, f32[384]{0:T(512)}, u32[]{:S(2)}) copy-start(f32[384]{0:T(512)} %param.18) | copy-start | bytes 4612
  75.1 659.4 %copy-start.46 = (f32[384]{0:T(512)S(1)}, f32[384]{0:T(512)}, u32[]{:S(2)}) copy-start(f32[384]{0:T(512)} %param.17) | copy-start | bytes 4612
  750.2 88.4 %copy-start.7 = (f32[384]{0:T(512)S(1)}, f32[384]{0:T(512)}, u32[]{:S(2)}) copy-start(f32[384]{0:T(512)} %copy-done.6) | copy-start | bytes 4612
  750.2 88.4 %copy-start.9 = (f32[384]{0:T(512)S(1)}, f32[384]{0:T(512)}, u32[]{:S(2)}) copy-start(f32[384]{0:T(512)} %copy-done.8) | copy-start | bytes 4612
  750.2 88.4 %copy-start.11 = (f32[384]{0:T(512)S(1)}, f32[384]{0:T(512)}, u32[]{:S(2)}) copy-start(f32[384]{0:T(512)} %copy-done.10) | copy-start | bytes 4612
  750.3 88.4 %copy-start.13 = (f32[384]{0:T(512)S(1)}, f32[384]{0:T(512)}, u32[]{:S(2)}) copy-start(f32[384]{0:T(512)} %copy-done.12) | copy-start | bytes 4612
  750.3 88.4 %copy-start.15 = (f32[384]{0:T(512)S(1)}, f32[384]{0:T(512)}, u32[]{:S(2)}) copy-start(f32[384]{0:T(512)} %copy-done.14) | copy-start | bytes 4612
  750.3 88.4 %copy-start.17 = (f32[384]{0:T(512)S(1)}, f32[384]{0:T(512)}, u32[]{:S(2)}) copy-start(f32[384]{0:T(512)} %copy-done.16) | copy-start | bytes 4612
  750.3 88.4 %copy-start.19 = (f32[384]{0:T(512)S(1)}, f32[384]{0:T(512)}, u32[]{:S(2)}) copy-start(f32[384]{0:T(512)} %copy-done.18) | copy-start | bytes 4612
  750.3 88.4 %copy-start.21 = (f32[384]{0:T(512)S(1)}, f32[384]{0:T(512)}, u32[]{:S(2)}) copy-start(f32[384]{0:T(512)} %copy-done.20) | copy-start | bytes 4612
  750.3 88.4 %copy-start.23 = (f32[384]{0:T(512)S(1)}, f32[384]{0:T(512)}, u32[]{:S(2)}) copy-start(f32[384]{0:T(512)} %copy-done.22) | copy-start | bytes 4612
  750.3 88.4 %copy-start.25 = (f32[384]{0:T(512)S(1)}, f32[384]{0:T(512)}, u32[]{:S(2)}) copy-start(f32[384]{0:T(512)} %copy-done.24) | copy-start | bytes 4612
  750.3 88.4 %copy-start.27 = (f32[384]{0:T(512)S(1)}, f32[384]{0:T(512)}, u32[]{:S(2)}) copy-start(f32[384]{0:T(512)} %copy-done.26) | copy-start | bytes 4612
  750.3 88.4 %copy-start.29 = (f32[384]{0:T(512)S(1)}, f32[384]{0:T(512)}, u32[]{:S(2)}) copy-start(f32[384]{0:T(512)} %copy-done.28) | copy-start | bytes 4612
  750.3 88.4 %copy-start.31 = (f32[384]{0:T(512)S(1)}, f32[384]{0:T(512)}, u32[]{:S(2)}) copy-start(f32[384]{0:T(512)} %copy-done.30) | copy-start | bytes 4612
  750.4 88.4 %copy-start.33 = (f32[384]{0:T(512)S(1)}, f32[384]{0:T(512)}, u32[]{:S(2)}) copy-start(f32[384]{0:T(512)} %copy-done.32) | copy-start | bytes 4612
  750.4 88.4 %copy-start.35 = (f32[384]{0:T(512)S(1)}, f32[384]{0:T(512)}, u32[]{:S(2)}) copy-start(f32[384]{0:T(512)} %copy-done.34) | copy-start | bytes 4612
  750.4 88.4 %copy-start.37 = (f32[384]{0:T(512)S(1)}, f32[384]{0:T(512)}, u32[]{:S(2)}) copy-start(f32[384]{0:T(512)} %copy-done.36) | copy-start | bytes 4612
  750.4 88.4 %copy-start.39 = (f32[384]{0:T(512)S(1)}, f32[384]{0:T(512)}, u32[]{:S(2)}) copy-start(f32[384]{0:T(512)} %copy-done.38) | copy-start | bytes 4612
  750.4 7.5 collective-permute-start.5
  752.4 6.5 collective-permute-start.4
  758.9 79.6 %collective-permute-start.7 = (bf16[14,3,384]{2,1,0:T(4,128)(2,1)S(1)}, bf16[14,3,384]{2,1,0:T(4,128)(2,1)S(1)}, u32[]{:S(2)}, u32[]{:S(2)}) collective-permute-start(bf16[14,3,384]{2,1,0:T(4,128)(2,1)S(1)} %get-tuple-element.118), channel_id=1, source_target_pairs={{1,0},{2,1},{3,2},{4,3},{5,4},{6,5},{7,6},{9,8},{10,9},{11,10},{12... | collective-permute-start | bytes 96776 | tf_op jit(solution)/shard_map/ppermute | solution.py:16
  760.9 77.6 %collective-permute-start.6 = (bf16[14,3,384]{2,1,0:T(4,128)(2,1)S(1)}, bf16[14,3,384]{2,1,0:T(4,128)(2,1)S(1)}, u32[]{:S(2)}, u32[]{:S(2)}) collective-permute-start(bf16[14,3,384]{2,1,0:T(4,128)(2,1)S(1)} %get-tuple-element.117), channel_id=1, source_target_pairs={{0,1},{1,2},{2,3},{3,4},{4,5},{5,6},{6,7},{8,9},{9,10},{10,11},{11... | collective-permute-start | bytes 96776 | tf_op jit(solution)/shard_map/ppermute | solution.py:15
  (26 other events, 204.1 us)
Sparse Core Ops, SparseCore 0:
  34.7 696.4 all-gather.2
  750.3 268.5 all-reduce.4
